TPU v7x, 1024 devices: a whole 4x4x32 slice. The times are simulated.
1024 devices in a mesh: row: 8 (over y_lo, x), col: 128 (over z, y_hi, core).
Axes of the slice: x: 4, y: 4 (y_hi: 2, y_lo: 2; y = y_hi * 2 + y_lo), z: 32, core: 2. Of those that a mesh axis runs over, the one named last changes fastest.
Arguments:
- view_a: bfloat16 [1024, 8192], P('col', 'row'), may hold values from -30 to 30
- view_b: bfloat16 [1024, 8192], P('row', 'col'), may hold values from -30 to 30
Outputs:
- loss: float32 [], replicated
- grad_a: bfloat16 [1024, 8192], P('col', 'row')
- grad_b: bfloat16 [1024, 8192], P('row', 'col')
All inputs are finite; a program needn't handle non-finite values.
Results may differ from a plain program's by a relative error of at most 0.0062.
Values may be sent and summed in bfloat16 or wider, within the bound.
A program may use at most 64 MiB of HBM per device.

v0:
```python
import functools

import jax
import jax.numpy as jnp
from jax import lax
from jax.sharding import Mesh
from jax.sharding import PartitionSpec as P

COL = ("col_0", "col_1", "col_2")
ROW = ("row_0", "row_1")
ROW_COL = ("row_0", "row_1", "col_0", "col_1", "col_2")


off_weight = 0.0051
epsilon = 1e-05


def joined_along(parts, dim):
    shape = list(parts.shape[1:])
    shape[dim] *= parts.shape[0]
    return jnp.moveaxis(parts, 0, dim).reshape(shape)


def stacked_from(shard, axes, order):
    parts = shard
    for k in order:
        parts = lax.all_gather(parts, axes[k])
    done = order[::-1]
    back = [done.index(k) for k in range(len(axes))]
    parts = parts.transpose(*back, *range(len(axes), parts.ndim))
    return parts.reshape(-1, *shard.shape)


def gathered_by_axis(shard, axes, order, dim):
    return joined_along(stacked_from(shard, axes, order), dim)


def sent_to_all(shard, axis):
    copies = jnp.broadcast_to(shard, (lax.axis_size(axis), *shard.shape))
    return lax.all_to_all(copies, axis, split_axis=0, concat_axis=0, tiled=True)


def gathered_copies(shard, axis, dim):
    return joined_along(sent_to_all(shard, axis), dim)


def reduced_to_own(parts, axes, order):
    shape = [lax.axis_size(a) for a in axes]
    parts = parts.reshape(*shape, *parts.shape[1:])
    parts = parts.transpose(*order, *range(len(axes), parts.ndim))
    parts = parts.reshape(-1, *parts.shape[len(axes) :])
    for k in order:
        parts = lax.psum_scatter(parts, axes[k], scatter_dimension=0, tiled=True)
    return parts[0]


def cut_along(shard, dim, count):
    shape = shard.shape
    parts = shard.reshape(*shape[:dim], count, shape[dim] // count, *shape[dim + 1 :])
    return jnp.moveaxis(parts, dim, 0)


def summed_rows(shard, axes, order, dim):
    count = lax.axis_size(axes)
    return reduced_to_own(cut_along(shard, dim, count), axes, order)


def summed_on_arrival(shard, axis, dim):
    parts = cut_along(shard, dim, lax.axis_size(axis))
    arrived = lax.all_to_all(parts, axis, split_axis=0, concat_axis=0, tiled=True)
    return arrived.sum(axis=0)


def one_axis_at_a_time(shard, axes):
    return functools.reduce(lax.psum, axes, shard)


def over_copies(shard, axis):
    return sent_to_all(shard, axis).sum(axis=0)


def packed_total(arrays, axis):
    ravelled, at, done = (jnp.concatenate([a.reshape(-1) for a in arrays]), 0, [])
    total = over_copies(ravelled, axis)
    for a in arrays:
        done.append(total[at : at + a.size].reshape(a.shape))
        at += a.size
    return tuple(done)


def normalize(values):
    values = values.astype(jnp.float32)
    center = jnp.mean(values, 0)
    spread = jnp.mean(jnp.square(values - center), 0)
    scaled = lax.rsqrt(spread + epsilon)
    return (((values - center) * scaled).astype(jnp.bfloat16), scaled)


def body(view_a, view_b):
    whole_a = gathered_by_axis(view_a, COL, (1, 0, 2), 0)
    whole_b = gathered_copies(view_b, ROW, 0)
    normed_a, scaled_a = normalize(whole_a)
    normed_b, scaled_b = normalize(whole_b)
    count = whole_a.shape[0]
    width_a = whole_a.shape[1]
    width_b = whole_b.shape[1]
    corr = (
        lax.dot_general(
            normed_a, normed_b, (((0,), (0,)), ((), ())), preferred_element_type=jnp.float32
        )
        / count
    )
    rows = lax.axis_index(ROW) * width_a + lax.iota(jnp.int32, width_a)
    columns = lax.axis_index(COL) * width_b + lax.iota(jnp.int32, width_b)
    diag = rows[:, None] == columns[None, :]
    partial_loss = jnp.sum(jnp.where(diag, jnp.square(1.0 - corr), off_weight * jnp.square(corr)))
    weights = jnp.where(diag, 2.0 * (corr - 1.0), 2.0 * off_weight * corr).astype(jnp.bfloat16)
    term_a = lax.dot_general(
        normed_b, weights, (((1,), (1,)), ((), ())), preferred_element_type=jnp.float32
    )
    term_b = jnp.dot(normed_a, weights, preferred_element_type=jnp.float32)
    summed_a = summed_rows(term_a, COL, (2, 0, 1), 0)
    summed_b = summed_on_arrival(term_b, ROW, 0)
    share_a = summed_a.shape[0]
    share_b = summed_b.shape[0]
    mine_a = lax.dynamic_slice_in_dim(normed_a, lax.axis_index(COL) * share_a, share_a, 0).astype(
        jnp.float32
    )
    mine_b = lax.dynamic_slice_in_dim(normed_b, lax.axis_index(ROW) * share_b, share_b, 0).astype(
        jnp.float32
    )
    first_a, second_a = (
        one_axis_at_a_time(jnp.sum(summed_a, 0), COL),
        one_axis_at_a_time(jnp.sum(summed_a * mine_a, 0), COL),
    )
    first_b, second_b = packed_total((jnp.sum(summed_b, 0), jnp.sum(summed_b * mine_b, 0)), ROW)
    grad_a = (scaled_a * (summed_a - first_a / count - mine_a * (second_a / count))).astype(
        jnp.bfloat16
    )
    grad_b = (scaled_b * (summed_b - first_b / count - mine_b * (second_b / count))).astype(
        jnp.bfloat16
    )
    total = one_axis_at_a_time(partial_loss, ROW_COL)
    loss = total / (width_a * lax.axis_size(ROW))
    return (loss, grad_a, grad_b)


def solution(mesh):
    split = Mesh(
        mesh.devices.reshape(2, 4, 32, 2, 2), ("row_0", "row_1", "col_0", "col_1", "col_2")
    )
    return jax.shard_map(
        body,
        mesh=split,
        in_specs=(P(COL, ROW), P(ROW, COL)),
        out_specs=(P(), P(COL, ROW), P(ROW, COL)),
        check_vma=False,
    )
```

profile of v0, /device:TPU:1, one launch (start us, length us, event | category | flops | bytes accessed | tf_op | source)
XLA Modules:
  0.0 487.1 jit_solution(10979397945724201108)
XLA Ops:
  7.2 7.1 %all-gather = bf16[16,1024]{1,0:T(8,128)(2,1)} all-gather(bf16[8,1024]{1,0:T(8,128)(2,1)} %param.2), channel_id=2, replica_groups=mesh['row_0'=2,'row_1'=4,'col_0'=32,'col_1'=2,'col_2'=2] {'col_1'}, dimensions={0}, use_global_device_ids=true | all-gather | bytes 49152 | tf_op jit(solution)/shard_map/all_gather | solution.py:27
  14.4 123.1 %all-gather.6.cloned.1.call-done = bf16[64,8,1024]{2,1,0:T(8,128)(2,1)} async-done(((bf16[2,8,1024]{2,1,0:T(8,128)(2,1)}), bf16[64,8,1024]{2,1,0:T(8,128)(2,1)}) %all-gather.6.cloned.1.call-update) | async-done | bytes 1048592 | tf_op jit(solution)/shard_map/all_gather | solution.py:27
  137.5 1.4 broadcast_in_dim.4
  138.9 4.9 %all-to-all-start = ((bf16[8,128,64]{1,2,0:T(8,128)(2,1)}), bf16[8,128,64]{1,2,0:T(8,128)(2,1)S(1)}, u32[]{:S(2)}, u32[]{:S(2)}) async-start(bf16[8,128,64]{1,2,0:T(8,128)(2,1)} %broadcast_in_dim.4), calls=%async_computation | async-start | bytes 262144 | tf_op jit(solution)/shard_map/all_to_all | solution.py:40
  143.9 5.3 %all-to-all-done = bf16[8,128,64]{1,2,0:T(8,128)(2,1)S(1)} async-done(((bf16[8,128,64]{1,2,0:T(8,128)(2,1)}), bf16[8,128,64]{1,2,0:T(8,128)(2,1)S(1)}, u32[]{:S(2)}, u32[]{:S(2)}) %all-to-all-start) | async-done | bytes 131104 | tf_op jit(solution)/shard_map/all_to_all | solution.py:40
  149.7 36.8 %all-gather.8.cloned.1.call-done = bf16[64,2,8,1024]{3,2,1,0:T(8,128)(2,1)} async-done(((bf16[32,2,8,1024]{3,2,1,0:T(8,128)(2,1)}), bf16[64,2,8,1024]{3,2,1,0:T(8,128)(2,1)}) %all-gather.8.cloned.1.call-update) | async-done | bytes 2097168 | tf_op jit(solution)/shard_map/all_gather | solution.py:27
  186.5 2.0 convert_reduce_fusion
  188.5 2.2 convert_element_type.103
  191.2 0.7 fusion
  191.9 0.8 copy-done
  193.0 1.2 fusion.4
  194.2 0.8 convolution_bitcast_fusion
  194.9 2.3 copy.42
  197.3 33.8 %reduce-scatter.4.cloned.1.call-done = f32[64,8,1024]{2,1,0:T(8,128)} async-done(((f32[128,8,1024]{2,1,0:T(8,128)}), f32[64,8,1024]{2,1,0:T(8,128)}) %reduce-scatter.4.cloned.1.call-update) | async-done | bytes 2097168 | tf_op jit(solution)/shard_map/reduce_scatter | solution.py:53
  231.1 2.5 copy.43
  233.6 1.9 copy-done.2
  235.5 1.5 fusion.1
  237.0 3.4 all-to-all-start.1
  240.4 7.3 %all-to-all-done.1 = f32[8,128,64]{1,2,0:T(8,128)S(1)} async-done(((f32[8,128,64]{1,2,0:T(8,128)}), f32[8,128,64]{1,2,0:T(8,128)S(1)}, u32[]{:S(2)}, u32[]{:S(2)}) %all-to-all-start.1) | async-done | bytes 262176 | tf_op jit(solution)/shard_map/all_to_all | solution.py:70
  248.1 0.6 broadcast_in_dim.5
  248.7 3.3 all-to-all-start.2
  252.1 4.5 psum.77
  256.6 9.3 %psum.78 = f32[]{:T(128)} all-reduce(f32[]{:T(128)} %psum.77), channel_id=1, replica_groups=mesh['row_0'=2,'row_1'=4,'col_0'=32,'col_1'=2,'col_2'=2] {'row_1'}, use_global_device_ids=true, to_apply=%region_6.7 | all-reduce | flops 1 | bytes 8 | tf_op jit(solution)/shard_map/psum | solution.py:75
  266.0 84.0 %reduce-scatter.6.cloned.1.call-done = f32[2,8,1024]{2,1,0:T(8,128)} async-done(((f32[64,8,1024]{2,1,0:T(8,128)}), f32[2,8,1024]{2,1,0:T(8,128)}) %reduce-scatter.6.cloned.1.call-update) | async-done | bytes 65552 | tf_op jit(solution)/shard_map/reduce_scatter | solution.py:53
  350.1 52.3 %reduce-scatter.8.cloned.1.call-done = f32[1,8,1024]{2,1,0:T(8,128)} async-done(((f32[2,8,1024]{2,1,0:T(8,128)}), f32[1,8,1024]{2,1,0:T(8,128)}) %reduce-scatter.8.cloned.1.call-update) | async-done | bytes 32784 | tf_op jit(solution)/shard_map/reduce_scatter | solution.py:53
  402.4 0.8 reduce_sum.104
  403.1 0.8 fusion.14
  403.9 0.7 fusion.21
  404.6 48.3 %all-reduce = (f32[]{:T(128)}, f32[1024]{0:T(1024)S(1)}, f32[1024]{0:T(1024)S(1)}) all-reduce(f32[]{:T(128)} %psum.78, f32[1024]{0:T(1024)S(1)} %fusion.14, f32[1024]{0:T(1024)S(1)} %reduce_sum.104), channel_id=1, replica_groups=mesh['row_0'=2,'row_1'=4,'col_0'=32,'col_1'=2,'col_2'=2] {'col_0'}, use_global_device_ids=true, to_apply=%region_7.8 | all-reduce | flops 2049 | bytes 16392 | tf_op jit(solution)/shard_map/psum | solution.py:75
  452.9 6.0 %all-reduce.2 = (f32[]{:T(128)}, f32[1024]{0:T(1024)S(1)}, f32[1024]{0:T(1024)S(1)}) all-reduce(f32[]{:T(128)} %get-tuple-element.5, f32[1024]{0:T(1024)S(1)} %get-tuple-element.6, f32[1024]{0:T(1024)S(1)} %get-tuple-element.7), channel_id=1, replica_groups=mesh['row_0'=2,'row_1'=4,'col_0'=32,'col_1'=2,'col_2'=2] {'col_1'}, use_global_device_ids=true, to_apply=%region_8.9 | all-reduce | flops 2049 | bytes 16392 | tf_op jit(solution)/shard_map/psum | solution.py:75
  458.9 18.4 %all-reduce.1 = (f32[]{:T(128)}, f32[1024]{0:T(1024)S(1)}, f32[1024]{0:T(1024)S(1)}) all-reduce(f32[]{:T(128)} %get-tuple-element.11, f32[1024]{0:T(1024)S(1)} %get-tuple-element.12, f32[1024]{0:T(1024)S(1)} %get-tuple-element.13), channel_id=1, replica_groups=mesh['row_0'=2,'row_1'=4,'col_0'=32,'col_1'=2,'col_2'=2] {'col_2'}, use_global_device_ids=true, to_apply=%region_9.10 | all-reduce | flops 2049 | bytes 16392 | tf_op jit(solution)/shard_map/psum | solution.py:75
  478.0 1.4 fusion.17
  (33 shorter events, 2.0 us)
Async XLA Ops:
  7.2 130.4 %all-gather.6.cloned.1.call-start = ((), (), s32[]{:S(2)}) async-start(), calls=%async_computation.9 | async-start | bytes 1081344 | tf_op jit(solution)/shard_map/all_gather | solution.py:27
  14.4 172.1 %all-gather.8.cloned.1.call-start = ((), (), s32[]{:S(2)}) async-start(), calls=%async_computation.10 | async-start | bytes 3145728 | tf_op jit(solution)/shard_map/all_gather | solution.py:27
  138.9 10.3 %all-to-all-start = ((bf16[8,128,64]{1,2,0:T(8,128)(2,1)}), bf16[8,128,64]{1,2,0:T(8,128)(2,1)S(1)}, u32[]{:S(2)}, u32[]{:S(2)}) async-start(bf16[8,128,64]{1,2,0:T(8,128)(2,1)} %broadcast_in_dim.4), calls=%async_computation | async-start | bytes 262144 | tf_op jit(solution)/shard_map/all_to_all | solution.py:40
  143.8 87.3 %reduce-scatter.4.cloned.1.call-start = ((), (), s32[]{:S(2)}) async-start(), calls=%async_computation.6 | async-start | bytes 6291456 | tf_op jit(solution)/shard_map/reduce_scatter | solution.py:53
  188.5 2.7 copy-start.1
  190.7 2.1 copy-start
  197.2 152.7 %reduce-scatter.6.cloned.1.call-start = ((), (), s32[]{:S(2)}) async-start(), calls=%async_computation.7 | async-start | bytes 2162688 | tf_op jit(solution)/shard_map/reduce_scatter | solution.py:53
  233.6 1.9 copy-start.2
  237.0 10.8 %all-to-all-start.1 = ((f32[8,128,64]{1,2,0:T(8,128)}), f32[8,128,64]{1,2,0:T(8,128)S(1)}, u32[]{:S(2)}, u32[]{:S(2)}) async-start(f32[8,128,64]{1,2,0:T(8,128)} %fusion.1), calls=%async_computation.4 | async-start | bytes 524288 | tf_op jit(solution)/shard_map/all_to_all | solution.py:70
  248.7 17.2 %all-to-all-start.2 = ((f32[8,1,128]{2,1,0:T(1,128)}), f32[8,1,128]{2,1,0:T(1,128)S(1)}, u32[]{:S(2)}, u32[]{:S(2)}) async-start(f32[8,1,128]{2,1,0:T(1,128)} %broadcast_in_dim.5), calls=%async_computation.5 | async-start | bytes 8192 | tf_op jit(solution)/shard_map/all_to_all | solution.py:40
  252.1 150.3 %reduce-scatter.8.cloned.1.call-start = ((), (), s32[]{:S(2)}) async-start(), calls=%async_computation.8 | async-start | bytes 98304 | tf_op jit(solution)/shard_map/reduce_scatter | solution.py:53
Sparse Core Ops, SparseCore 0:
  14.5 122.9 all-gather.5
  140.2 46.2 all-gather.7
  197.4 33.6 reduce-scatter.3
  234.3 115.6 reduce-scatter.5
  353.1 49.1 reduce-scatter.7
where the time goes:
time: 488 us; the launch traced here: 487 us
  waiting for transfers between devices  343 us (70%)
  blocking collectives  93.7 us (19%)
  between operations  15.7 us (3%)
  starting transfers between devices  11.8 us (2%)
  local copies, waits for them, and re-layouts  9.92 us (2%)
  other arithmetic  9.89 us (2%)
    reduce_scatter x3, waiting for transfers between devices, reduced_to_own(): parts = lax.psum_scatter(parts, axes[k], scatter_dimension=0, tiled=True)  170 us
    all_gather x2, waiting for transfers between devices, stacked_from(): parts = lax.all_gather(parts, axes[k])  160 us
    psum x5, blocking collectives, one_axis_at_a_time(): return functools.reduce(lax.psum, axes, shard)  86.5 us
  transfers between devices with their start and end apart: 8, of which 7 were waited for; matrix products, arithmetic and copies ran while one was open for 1% of the time, Pallas kernels for 0%

commit v1 on v0

v1 whole, which is shorter than its diff:
```python
import functools

import jax
import jax.numpy as jnp
from jax import lax
from jax.experimental import pallas as pl
from jax.experimental.pallas import tpu as pltpu
from jax.sharding import Mesh
from jax.sharding import PartitionSpec as P

AXES = ("yl", "x", "z", "yh", "k")
ROW = ("yl", "x")
COL = ("z", "yh", "k")
MESH = pl.DeviceIdType.MESH

off_weight = 0.0051
epsilon = 1e-05
K = 2
LANES = 128
SUB = 8

f32 = jnp.float32
bf16 = jnp.bfloat16


def kernel(
    X, ZL, YH, ZH,
    a_ref, b_ref, loss_ref, ga_ref, gb_ref,
    ta, xa, pb, xf, na, nb,
    gp_a, gp_b, ra_a, ra_b, hs_a, hs_b, rb_a, rb_b, ms_a, ms_b, rg_a, rg_b,
    ds0, db0, ds1, db1, ss_a, sb_a, ss_b, sb_b, fs, fa, tb, tp,
    send, recv,
):
    R, M = ZH, ZL * YH
    N = R * K
    rows = M * SUB
    images = N * rows
    features = ZH * M * LANES
    yl, x, z, yh, k = (lax.axis_index(name) for name in AXES)
    r = yl * X + x
    zh, zl = z // ZL, z % ZL
    rho, m = r * K + k, zl * YH + yh
    s = m * K + k

    def device(r_, z_, yh_, k_):
        return (r_ // X, r_ % X, z_, yh_, k_)

    def near_row(p):
        return device(p // K, z, yh, p % K)

    def near_chip(p):
        return device(r, zh * ZL + p // YH, p % YH, k)

    def far_block(p):
        return device(r, p * ZL + zl, yh, k)

    def target(q):
        return device(zh, r * ZL + q // YH, q % YH, s // M)

    def source(b):
        s_ = k * M + b
        return device(zh, r * ZL + (s_ // K) // YH, (s_ // K) % YH, s_ % K)

    own = jnp.logical_and(zh == r, s // M == k)
    own_target, own_source = m, s % M

    barrier = pltpu.get_barrier_semaphore()

    def greet(n, me, peer):
        def one(t, c):
            pl.semaphore_signal(barrier, inc=1, device_id=peer(lax.rem(me + t, n)), device_id_type=MESH)
            return c

        lax.fori_loop(1, n, one, 0)

    def greet_across(peer, own_index):
        def one(q, c):
            @pl.when(jnp.logical_not(jnp.logical_and(own, q == own_index)))
            def _():
                pl.semaphore_signal(barrier, inc=1, device_id=peer(q), device_id_type=MESH)

            return c

        lax.fori_loop(0, M, one, 0)

    greet_across(target, own_target)
    greet_across(source, own_source)
    greet(ZH, zh, far_block)
    greet(M, m, near_chip)
    greet(N, rho, near_row)
    pl.semaphore_wait(barrier, 2 * M + (ZH - 1) + (M - 1) + (N - 1) - 2 * own.astype(jnp.int32))

    def spread(n, me, peer, src, dst, i):
        def one(t, c):
            p = lax.rem(me + t, n)
            pltpu.make_async_remote_copy(
                src_ref=src(p), dst_ref=dst.at[me], send_sem=send.at[i], recv_sem=recv.at[i],
                device_id=peer(p), device_id_type=MESH,
            ).start()
            return c

        lax.fori_loop(1, n, one, 0)
        pltpu.make_async_copy(src(me), dst.at[me], recv.at[i]).start()

    def arrived(dst, i):
        pltpu.make_async_copy(dst, dst, recv.at[i]).wait()

    def sent(dst, n, i):
        part = dst.at[pl.ds(0, n)]
        pltpu.make_async_copy(part, part, send.at[i]).wait()

    def across(peer, own_index, src, dst, slot, i):
        def one(q, c):
            mine = jnp.logical_and(own, q == own_index)

            @pl.when(mine)
            def _():
                pltpu.make_async_copy(src(q), dst.at[slot], recv.at[i]).start()

            @pl.when(jnp.logical_not(mine))
            def _():
                pltpu.make_async_remote_copy(
                    src_ref=src(q), dst_ref=dst.at[slot], send_sem=send.at[i], recv_sem=recv.at[i],
                    device_id=peer(q), device_id_type=MESH,
                ).start()

            return c

        lax.fori_loop(0, M, one, 0)

    def sent_across(dst, i):
        @pl.when(own)
        def _():
            sent(dst, M - 1, i)

        @pl.when(jnp.logical_not(own))
        def _():
            sent(dst, M, i)

    def columns(q):
        return a_ref.at[:, pl.ds(pl.multiple_of(q * LANES, LANES), LANES)]

    across(target, own_target, columns, ta, own_source, 0)
    spread(N, rho, near_row, lambda p: b_ref, pb, 1)

    def normalize(normed):
        values = xf[...]
        center = jnp.sum(values, 0, keepdims=True) / images
        shifted = values - center
        spread_ = jnp.sum(shifted * shifted, 0, keepdims=True) / images
        scaled = lax.rsqrt(spread_ + epsilon)
        normed[...] = (shifted * scaled).astype(bf16)
        return scaled

    own_rows = pl.ds(pl.multiple_of(rho * rows, rows), rows)

    def gram(normed, out):
        g = lax.dot_general(
            normed[own_rows, :], normed[...], (((1,), (1,)), ((), ())), preferred_element_type=f32
        )
        out[...] = g.reshape(M, SUB, images).astype(bf16)

    def summed(parts):
        return functools.reduce(jnp.add, [parts[i].astype(f32) for i in range(parts.shape[0])])

    arrived(pb, 1)
    low = lax.broadcasted_iota(jnp.int32, (rows, LANES), 1) < LANES // 2
    for i in range(R):
        p0, p1 = pb[2 * i].astype(f32), pb[2 * i + 1].astype(f32)
        xf[pl.ds(2 * i * rows, rows), :] = jnp.where(low, p0, pltpu.roll(p1, LANES // 2, 1))
        xf[pl.ds((2 * i + 1) * rows, rows), :] = jnp.where(low, pltpu.roll(p0, LANES // 2, 1), p1)
    scaled_b = normalize(nb)
    gram(nb, gp_b)
    spread(M, m, near_chip, lambda p: gp_b.at[p], ra_b, 2)

    arrived(ta, 0)
    spread(N, rho, near_row, lambda p: ta, xa, 3)

    arrived(ra_b, 2)
    hs_b[...] = summed(ra_b).astype(bf16)
    spread(ZH, zh, far_block, lambda p: hs_b, rb_b, 4)

    arrived(xa, 3)
    for i in range(N):
        xf[pl.ds(i * rows, rows), :] = xa[i].astype(f32).reshape(rows, LANES)
    scaled_a = normalize(na)
    gram(na, gp_a)
    spread(M, m, near_chip, lambda p: gp_a.at[p], ra_a, 5)

    corr = jnp.sum(na[...].astype(f32) * nb[...].astype(f32), 0, keepdims=True) / images
    d = 2.0 * (corr - 1.0) - (2.0 * off_weight) * corr
    ds0[...] = jnp.broadcast_to(jnp.square(1.0 - corr) - off_weight * jnp.square(corr), ds0.shape)
    spread(M, m, near_chip, lambda p: ds0, db0, 6)

    arrived(ra_a, 5)
    hs_a[...] = summed(ra_a).astype(bf16)
    spread(ZH, zh, far_block, lambda p: hs_a, rb_a, 7)

    arrived(db0, 6)
    ds1[...] = summed(db0)
    spread(ZH, zh, far_block, lambda p: ds1, db1, 8)

    arrived(rb_b, 4)
    ms_b[...] = summed(rb_b).astype(bf16)
    spread(M, m, near_chip, lambda p: ms_b, rg_b, 9)

    mine_a, mine_b = na[own_rows, :].astype(f32), nb[own_rows, :].astype(f32)
    line = lax.broadcasted_iota(jnp.int32, (SUB, LANES), 0)

    def term_of(rg, normed, other):
        g = rg[...].astype(f32).reshape(rows, images)
        product = jnp.dot(g.astype(bf16), normed[...], preferred_element_type=f32)
        return (2.0 * off_weight / images) * product + other * d, g

    def tile_of(*lines):
        out = jnp.zeros((SUB, LANES), f32)
        for i, v in enumerate(lines):
            out = jnp.where(line == i, jnp.broadcast_to(v, out.shape), out)
        return out

    def projected(term, mine, scaled, first, second):
        return scaled * (term - first / images - mine * (second / images))

    arrived(rg_b, 9)
    term_a, g_b = term_of(rg_b, na, mine_b)
    ss_a[...] = tile_of(jnp.sum(term_a, 0, keepdims=True), jnp.sum(term_a * mine_a, 0, keepdims=True))
    spread(N, rho, near_row, lambda p: ss_a, sb_a, 10)

    arrived(sb_a, 10)
    sums = summed(sb_a)
    grad_a = projected(term_a, mine_a, scaled_a, sums[0:1], sums[1:2])
    fs[...] = grad_a.reshape(M, SUB, LANES).astype(bf16)
    across(source, own_source, lambda b: fs.at[b], fa, own_target, 11)

    arrived(rb_a, 7)
    ms_a[...] = summed(rb_a).astype(bf16)
    spread(M, m, near_chip, lambda p: ms_a, rg_a, 12)
    arrived(rg_a, 12)
    term_b, g_a = term_of(rg_a, nb, mine_a)
    both = jnp.sum(g_a * g_b, 0, keepdims=True)
    trace = functools.reduce(jnp.add, [both[:, i * LANES : (i + 1) * LANES] for i in range(images // LANES)])
    ss_b[...] = tile_of(
        jnp.sum(term_b, 0, keepdims=True), jnp.sum(term_b * mine_b, 0, keepdims=True), trace
    )
    spread(N, rho, near_row, lambda p: ss_b, sb_b, 13)
    arrived(sb_b, 13)
    sums = summed(sb_b)
    grad_b = projected(term_b, mine_b, scaled_b, sums[0:1], sums[1:2])
    tb[...] = grad_b.astype(bf16)
    partner = pltpu.make_async_remote_copy(
        src_ref=tb, dst_ref=tp, send_sem=send.at[14], recv_sem=recv.at[14],
        device_id=device(r, z, yh, 1 - k), device_id_type=MESH,
    )
    partner.start()

    arrived(db1, 8)
    diagonal = summed(db1)[0:1]
    each = diagonal + sums[2:3] * (off_weight / (images * images))
    loss_ref[...] = jnp.broadcast_to(jnp.sum(each, 1, keepdims=True) / features, loss_ref.shape)

    partner.wait()
    other = tp[...].astype(f32)
    first_half = jnp.where(low, grad_b, pltpu.roll(other, LANES // 2, 1))
    second_half = jnp.where(low, pltpu.roll(other, LANES // 2, 1), grad_b)
    gb_ref[...] = jnp.where(k == 0, first_half, second_half).astype(bf16)

    arrived(fa, 11)
    for q in range(M):
        ga_ref[:, q * LANES : (q + 1) * LANES] = fa[q]

    sent_across(ta, 0)
    sent_across(fa, 11)
    for i, dst in ((1, pb), (3, xa), (10, sb_a), (13, sb_b)):
        sent(dst, N - 1, i)
    for i, dst in ((2, ra_b), (5, ra_a), (6, db0), (9, rg_b), (12, rg_a)):
        sent(dst, M - 1, i)
    for i, dst in ((4, rb_b), (7, rb_a), (8, db1)):
        sent(dst, ZH - 1, i)


def solution_on(split, interpret=False):
    YL, X, Z, YH, _ = split.devices.shape
    R = YL * X
    ZH, ZL = R, Z // R
    M, N = ZL * YH, R * K
    rows = M * SUB
    images = N * rows

    def body(view_a, view_b):
        packed = jnp.concatenate([view_b[:rows], view_b[rows:]], axis=1)
        vmem = pltpu.VMEM
        loss, grad_a, packed_b = pl.pallas_call(
            functools.partial(kernel, X, ZL, YH, ZH),
            out_shape=(
                jax.ShapeDtypeStruct((SUB, LANES), f32),
                jax.ShapeDtypeStruct(view_a.shape, bf16),
                jax.ShapeDtypeStruct(packed.shape, bf16),
            ),
            in_specs=[pl.BlockSpec(memory_space=pltpu.VMEM)] * 2,
            out_specs=[pl.BlockSpec(memory_space=pltpu.VMEM)] * 3,
            scratch_shapes=[
                vmem((M, SUB, LANES), bf16),
                vmem((N, M, SUB, LANES), bf16),
                vmem((N, rows, LANES), bf16),
                vmem((images, LANES), f32),
                vmem((images, LANES), bf16),
                vmem((images, LANES), bf16),
                vmem((M, SUB, images), bf16),
                vmem((M, SUB, images), bf16),
                vmem((M, SUB, images), bf16),
                vmem((M, SUB, images), bf16),
                vmem((SUB, images), bf16),
                vmem((SUB, images), bf16),
                vmem((ZH, SUB, images), bf16),
                vmem((ZH, SUB, images), bf16),
                vmem((SUB, images), bf16),
                vmem((SUB, images), bf16),
                vmem((M, SUB, images), bf16),
                vmem((M, SUB, images), bf16),
                vmem((SUB, LANES), f32),
                vmem((M, SUB, LANES), f32),
                vmem((SUB, LANES), f32),
                vmem((ZH, SUB, LANES), f32),
                vmem((SUB, LANES), f32),
                vmem((N, SUB, LANES), f32),
                vmem((SUB, LANES), f32),
                vmem((N, SUB, LANES), f32),
                vmem((M, SUB, LANES), bf16),
                vmem((M, SUB, LANES), bf16),
                vmem((rows, LANES), bf16),
                vmem((rows, LANES), bf16),
                pltpu.SemaphoreType.DMA((15,)),
                pltpu.SemaphoreType.DMA((15,)),
            ],
            compiler_params=pltpu.CompilerParams(collective_id=0, has_side_effects=True),
            interpret=interpret,
        )(view_a, packed)
        half = LANES // K
        grad_b = jnp.concatenate([packed_b[:, :half], packed_b[:, half:]], axis=0)
        return loss[0, 0], grad_a, grad_b

    return jax.shard_map(
        body,
        mesh=split,
        in_specs=(P(COL, ROW), P(ROW, COL)),
        out_specs=(P(), P(COL, ROW), P(ROW, COL)),
        check_vma=False,
    )


def solution(mesh):
    return solution_on(Mesh(mesh.devices.reshape(2, 4, 32, 2, 2), AXES))
```

time: 488 us -> 104 us (0.21)
  waiting for transfers between devices: 343 us -> 0 us
  Pallas kernels: 0 us -> 97.4 us
  blocking collectives: 93.7 us -> 0 us
  between operations: 15.7 us -> 0.66 us
  starting transfers between devices: 11.8 us -> 0 us
  other arithmetic: 9.89 us -> 0.71 us
  local copies, waits for them, and re-layouts: 9.92 us -> 4.43 us
    reduce_scatter x3 -> x0, waiting for transfers between devices: 170 us -> none  [reduced_to_own(): parts = lax.psum_scatter(parts, axes[k], scatter_dimension=0, tiled=True)]
    all_gather x2 -> x0, waiting for transfers between devices: 160 us -> none  [stacked_from(): parts = lax.all_gather(parts, axes[k])]
    pallas_call x0 -> x1, Pallas kernels: none -> 97.4 us  [body(): pl.pallas_call(functools.partial(kernel, X, ZL, YH, ZH), out_shape=(jax.S...]
    psum x5 -> x0, blocking collectives: 86.5 us -> none  [one_axis_at_a_time(): return functools.reduce(lax.psum, axes, shard)]
    all_to_all x3 -> x0, waiting for transfers between devices: 12.7 us -> none  [the longest x1 7.33 us: summed_on_arrival(): lax.all_to_all(parts, axis, split_axis=0, concat_axis=0, tiled=True)]
    all_to_all x3 -> x0, starting transfers between devices: 11.6 us -> none  [the longest x2 8.2 us: sent_to_all(): return lax.all_to_all(copies, axis, split_axis=0, concat_axis=0, tiled=True)]
    all_gather x1 -> x0, blocking collectives: 7.14 us -> none  [stacked_from(): parts = lax.all_gather(parts, axes[k])]
  transfers between devices with their start and end apart: 8 -> 0, of which waited for: 7 -> 0; matrix products, arithmetic and copies ran while one was open for 1% -> 0% of each run, Pallas kernels for 0% -> 0%
where the time goes in v1:
time: 104 us; the launch traced here: 103 us
  Pallas kernels  97.4 us (94%)
  local copies, waits for them, and re-layouts  4.43 us (4%)
    pallas_call x1, Pallas kernels, body(): pl.pallas_call(functools.partial(kernel, X, ZL, YH, ZH), out_shape=(jax.S...  97.4 us

profile of v1, /device:TPU:1, one launch (start us, length us, event | category | flops | bytes accessed | tf_op | source)
XLA Modules:
  0.0 103.2 jit_solution(8273317727873548584)
XLA Ops:
  0.6 0.9 fusion.1
  1.5 0.1 copy.8
  1.6 0.1 copy.9
  1.7 0.7 pad_maximum_fusion.1.b_ref
  2.4 97.4 %shard_map.49 = (f32[8,128]{1,0:T(8,128)}, bf16[8,1024]{1,0:T(8,128)(2,1)}, bf16[64,128]{1,0:T(8,128)(2,1)}) custom-call(bf16[8,1024]{1,0:T(8,128)(2,1)} %a_ref.1, bf16[64,128]{1,0:T(8,128)(2,1)} %pad_maximum_fusion.1.b_ref), custom_call_target="tpu_custom_call" | custom-call | tf_op jit(solution)/shard_map/pallas_call | solution.py:292
  99.8 1.2 %slice.17 = f32[1,1]{1,0:T(1,128)} slice(f32[8,128]{1,0:T(8,128)} %get-tuple-element.6), slice={[0:1], [0:1]} | slice | bytes 8 | tf_op jit(solution)/shard_map/slice | solution.py:340
  101.0 0.9 fusion
  101.9 0.0 copy-start
  101.9 0.7 copy.7
  102.6 0.0 copy-done
  102.6 0.6 copy.11
  (1 shorter events, 0.0 us)
Async XLA Ops:
  101.9 0.7 copy-start

commit v2 on v1

--- a/solution.py
+++ b/solution.py
@@ -25,11 +25,11 @@
 
 def kernel(
     X, ZL, YH, ZH,
-    a_ref, b_ref, loss_ref, ga_ref, gb_ref,
-    ta, xa, pb, xf, na, nb,
+    a_ref, view_ref, loss_ref, ga_ref, gb_ref,
+    b_ref, ta, xa, pb, xf, na, nb,
     gp_a, gp_b, ra_a, ra_b, hs_a, hs_b, rb_a, rb_b, ms_a, ms_b, rg_a, rg_b,
     ds0, db0, ds1, db1, ss_a, sb_a, ss_b, sb_b, fs, fa, tb, tp,
-    send, recv,
+    send, recv, ring, hop,
 ):
     R, M = ZH, ZL * YH
     N = R * K
@@ -64,6 +64,10 @@
     own = jnp.logical_and(zh == r, s // M == k)
     own_target, own_source = m, s % M
 
+    half = LANES // K
+    view_b = view_ref[...].astype(f32).T
+    b_ref[...] = jnp.concatenate([view_b[:rows], view_b[rows:]], axis=1).astype(bf16)
+
     barrier = pltpu.get_barrier_semaphore()
 
     def greet(n, me, peer):
@@ -88,7 +92,8 @@
     greet(ZH, zh, far_block)
     greet(M, m, near_chip)
     greet(N, rho, near_row)
-    pl.semaphore_wait(barrier, 2 * M + (ZH - 1) + (M - 1) + (N - 1) - 2 * own.astype(jnp.int32))
+    with jax.named_scope("s0_barrier"):
+        pl.semaphore_wait(barrier, 2 * M + (ZH - 1) + (M - 1) + (N - 1) - 2 * own.astype(jnp.int32))
 
     def spread(n, me, peer, src, dst, i):
         def one(t, c):
@@ -103,7 +108,8 @@
         pltpu.make_async_copy(src(me), dst.at[me], recv.at[i]).start()
 
     def arrived(dst, i):
-        pltpu.make_async_copy(dst, dst, recv.at[i]).wait()
+        with jax.named_scope(f"w{i}"):
+            pltpu.make_async_copy(dst, dst, recv.at[i]).wait()
 
     def sent(dst, n, i):
         part = dst.at[pl.ds(0, n)]
@@ -136,6 +142,38 @@
         @pl.when(jnp.logical_not(own))
         def _():
             sent(dst, M, i)
+
+    up, down = ZH // 2, ZH - 1 - ZH // 2
+
+    def pass_on(src, dst, slot, i, j, step):
+        pltpu.make_async_remote_copy(
+            src_ref=src, dst_ref=dst.at[slot], send_sem=ring.at[i], recv_sem=hop.at[i, j],
+            device_id=far_block(lax.rem(zh + step + ZH, ZH)), device_id_type=MESH,
+        ).start()
+
+    def came(dst, slot, i, j):
+        with jax.named_scope(f"h{i}_{j}"):
+            pltpu.make_async_copy(dst.at[slot], dst.at[slot], hop.at[i, j]).wait()
+
+    def ring_start(src, dst, i):
+        pltpu.make_async_copy(src, dst.at[zh], hop.at[i, 0]).start()
+        pass_on(src, dst, zh, i, 1, 1)
+        if down:
+            pass_on(src, dst, zh, i, up + 1, -1)
+
+    def ring_step(dst, i, j):
+        if j <= up:
+            slot = lax.rem(zh - j + ZH, ZH)
+            came(dst, slot, i, j)
+            if j < up:
+                pass_on(dst.at[slot], dst, slot, i, j + 1, 1)
+        if j <= down:
+            slot = lax.rem(zh + j, ZH)
+            came(dst, slot, i, up + j)
+            if j < down:
+                pass_on(dst.at[slot], dst, slot, i, up + j + 1, -1)
+        if j == up:
+            came(dst, zh, i, 0)
 
     def columns(q):
         return a_ref.at[:, pl.ds(pl.multiple_of(q * LANES, LANES), LANES)]
@@ -173,12 +211,14 @@
     gram(nb, gp_b)
     spread(M, m, near_chip, lambda p: gp_b.at[p], ra_b, 2)
 
+    arrived(ra_b, 2)
+    hs_b[...] = summed(ra_b).astype(bf16)
+    ring_start(hs_b, rb_b, 0)
+
     arrived(ta, 0)
     spread(N, rho, near_row, lambda p: ta, xa, 3)
-
-    arrived(ra_b, 2)
-    hs_b[...] = summed(ra_b).astype(bf16)
-    spread(ZH, zh, far_block, lambda p: hs_b, rb_b, 4)
+    for j in range(1, up):
+        ring_step(rb_b, 0, j)
 
     arrived(xa, 3)
     for i in range(N):
@@ -194,18 +234,20 @@
 
     arrived(ra_a, 5)
     hs_a[...] = summed(ra_a).astype(bf16)
-    spread(ZH, zh, far_block, lambda p: hs_a, rb_a, 7)
+    ring_start(hs_a, rb_a, 1)
+
+    ring_step(rb_b, 0, up)
+    ms_b[...] = summed(rb_b).astype(bf16)
+    spread(M, m, near_chip, lambda p: ms_b, rg_b, 9)
 
     arrived(db0, 6)
     ds1[...] = summed(db0)
     spread(ZH, zh, far_block, lambda p: ds1, db1, 8)
 
-    arrived(rb_b, 4)
-    ms_b[...] = summed(rb_b).astype(bf16)
-    spread(M, m, near_chip, lambda p: ms_b, rg_b, 9)
-
     mine_a, mine_b = na[own_rows, :].astype(f32), nb[own_rows, :].astype(f32)
     line = lax.broadcasted_iota(jnp.int32, (SUB, LANES), 0)
+    if up > 1:
+        ring_step(rb_a, 1, 1)
 
     def term_of(rg, normed, other):
         g = rg[...].astype(f32).reshape(rows, images)
@@ -226,13 +268,18 @@
     ss_a[...] = tile_of(jnp.sum(term_a, 0, keepdims=True), jnp.sum(term_a * mine_a, 0, keepdims=True))
     spread(N, rho, near_row, lambda p: ss_a, sb_a, 10)
 
+    for j in range(2, up - 1):
+        ring_step(rb_a, 1, j)
+
     arrived(sb_a, 10)
     sums = summed(sb_a)
     grad_a = projected(term_a, mine_a, scaled_a, sums[0:1], sums[1:2])
     fs[...] = grad_a.reshape(M, SUB, LANES).astype(bf16)
     across(source, own_source, lambda b: fs.at[b], fa, own_target, 11)
 
-    arrived(rb_a, 7)
+    for j in range(max(up - 1, 2), up):
+        ring_step(rb_a, 1, j)
+    ring_step(rb_a, 1, up)
     ms_a[...] = summed(rb_a).astype(bf16)
     spread(M, m, near_chip, lambda p: ms_a, rg_a, 12)
     arrived(rg_a, 12)
@@ -256,13 +303,14 @@
     arrived(db1, 8)
     diagonal = summed(db1)[0:1]
     each = diagonal + sums[2:3] * (off_weight / (images * images))
-    loss_ref[...] = jnp.broadcast_to(jnp.sum(each, 1, keepdims=True) / features, loss_ref.shape)
-
-    partner.wait()
+    loss_ref[0, 0] = jnp.sum(each) / features
+
+    with jax.named_scope("w14"):
+        partner.wait()
     other = tp[...].astype(f32)
-    first_half = jnp.where(low, grad_b, pltpu.roll(other, LANES // 2, 1))
-    second_half = jnp.where(low, pltpu.roll(other, LANES // 2, 1), grad_b)
-    gb_ref[...] = jnp.where(k == 0, first_half, second_half).astype(bf16)
+    turned, other_turned = pltpu.roll(grad_b, half, 1), pltpu.roll(other, half, 1)
+    gb_ref[:rows, :] = jnp.where(k == 0, grad_b, other_turned)[:, :half].astype(bf16)
+    gb_ref[rows:, :] = jnp.where(k == 0, other, turned)[:, :half].astype(bf16)
 
     arrived(fa, 11)
     for q in range(M):
@@ -274,8 +322,10 @@
         sent(dst, N - 1, i)
     for i, dst in ((2, ra_b), (5, ra_a), (6, db0), (9, rg_b), (12, rg_a)):
         sent(dst, M - 1, i)
-    for i, dst in ((4, rb_b), (7, rb_a), (8, db1)):
-        sent(dst, ZH - 1, i)
+    for i, dst in ((0, rb_b), (1, rb_a)):
+        part = dst.at[pl.ds(0, ZH - 1)]
+        pltpu.make_async_copy(part, part, ring.at[i]).wait()
+    sent(db1, ZH - 1, 8)
 
 
 def solution_on(split, interpret=False):
@@ -287,18 +337,22 @@
     images = N * rows
 
     def body(view_a, view_b):
-        packed = jnp.concatenate([view_b[:rows], view_b[rows:]], axis=1)
         vmem = pltpu.VMEM
-        loss, grad_a, packed_b = pl.pallas_call(
+        loss, grad_a, grad_b = pl.pallas_call(
             functools.partial(kernel, X, ZL, YH, ZH),
             out_shape=(
-                jax.ShapeDtypeStruct((SUB, LANES), f32),
+                jax.ShapeDtypeStruct((1, 1), f32),
                 jax.ShapeDtypeStruct(view_a.shape, bf16),
-                jax.ShapeDtypeStruct(packed.shape, bf16),
+                jax.ShapeDtypeStruct(view_b.shape, bf16),
             ),
             in_specs=[pl.BlockSpec(memory_space=pltpu.VMEM)] * 2,
-            out_specs=[pl.BlockSpec(memory_space=pltpu.VMEM)] * 3,
+            out_specs=[
+                pl.BlockSpec(memory_space=pltpu.SMEM),
+                pl.BlockSpec(memory_space=pltpu.VMEM),
+                pl.BlockSpec(memory_space=pltpu.VMEM),
+            ],
             scratch_shapes=[
+                vmem((rows, LANES), bf16),
                 vmem((M, SUB, LANES), bf16),
                 vmem((N, M, SUB, LANES), bf16),
                 vmem((N, rows, LANES), bf16),
@@ -331,13 +385,13 @@
                 vmem((rows, LANES), bf16),
                 pltpu.SemaphoreType.DMA((15,)),
                 pltpu.SemaphoreType.DMA((15,)),
+                pltpu.SemaphoreType.DMA((2,)),
+                pltpu.SemaphoreType.DMA((2, ZH)),
             ],
             compiler_params=pltpu.CompilerParams(collective_id=0, has_side_effects=True),
             interpret=interpret,
-        )(view_a, packed)
-        half = LANES // K
-        grad_b = jnp.concatenate([packed_b[:, :half], packed_b[:, half:]], axis=0)
-        return loss[0, 0], grad_a, grad_b
+        )(view_a, view_b.T)
+        return loss.reshape(()), grad_a, grad_b
 
     return jax.shard_map(
         body,

time: 104 us -> 103 us (level)
  local copies, waits for them, and re-layouts: 4.43 us -> 2.07 us
  between operations: 0.66 us -> 2.41 us
    slice x3 -> x0, local copies, waits for them, and re-layouts: 2.93 us -> none  [the longest x1 1.2 us: body(): return (loss[0, 0], grad_a, grad_b)]
where the time goes in v2:
time: 103 us; the launch traced here: 102 us
  Pallas kernels  97.9 us (95%)
  between operations  2.41 us (2%)
  local copies, waits for them, and re-layouts  2.07 us (2%)
    pallas_call x1, Pallas kernels, body(): pl.pallas_call(functools.partial(kernel, X, ZL, YH, ZH), out_shape=(jax.S...  97.9 us
    unnamed x4, local copies, waits for them, and re-layouts  2.07 us

profile of v2, /device:TPU:1, one launch (start us, length us, event | category | flops | bytes accessed | tf_op | source)
XLA Modules:
  0.0 102.4 jit_solution(11183764924148771926)
XLA Ops:
  0.6 97.9 %shard_map.49 = (f32[1,1]{1,0:T(1,128)}, bf16[8,1024]{1,0:T(8,128)(2,1)}, bf16[128,64]{1,0:T(8,128)(2,1)}) custom-call(bf16[8,1024]{1,0:T(8,128)(2,1)} %a_ref.1, bf16[64,128]{1,0:T(8,128)(2,1)} %bitcast.2), custom_call_target="tpu_custom_call" | custom-call | tf_op jit(solution)/shard_map/pallas_call | solution.py:341
  98.5 0.0 copy-start
  98.6 1.5 %copy.5 = bf16[128,64]{0,1:T(8,128)(2,1)} copy(bf16[128,64]{1,0:T(8,128)(2,1)} %get-tuple-element.11) | data formatting | bytes 32768
  100.6 0.0 copy-done
  100.6 0.6 copy.9
Async XLA Ops:
  98.5 2.1 %copy-start = (bf16[8,1024]{1,0:T(8,128)(2,1)S(1)}, bf16[8,1024]{1,0:T(8,128)(2,1)}, u32[]{:S(2)}) copy-start(bf16[8,1024]{1,0:T(8,128)(2,1)} %get-tuple-element.16) | copy-start | bytes 49156

commit v3 on v2

--- a/solution.py
+++ b/solution.py
@@ -26,9 +26,9 @@
 def kernel(
     X, ZL, YH, ZH,
     a_ref, view_ref, loss_ref, ga_ref, gb_ref,
-    b_ref, ta, xa, pb, xf, na, nb,
+    a_in, view_in, b_ref, ta, xa, pb, xf, na, nb,
     gp_a, gp_b, ra_a, ra_b, hs_a, hs_b, rb_a, rb_b, ms_a, ms_b, rg_a, rg_b,
-    ds0, db0, ds1, db1, ss_a, sb_a, ss_b, sb_b, fs, fa, tb, tp,
+    ss_a, sb_a, ss_b, sb_b, ls, lb, fs, fa, tb, tp,
     send, recv, ring, hop,
 ):
     R, M = ZH, ZL * YH
@@ -65,8 +65,10 @@
     own_target, own_source = m, s % M
 
     half = LANES // K
-    view_b = view_ref[...].astype(f32).T
-    b_ref[...] = jnp.concatenate([view_b[:rows], view_b[rows:]], axis=1).astype(bf16)
+    fetch_a = pltpu.make_async_copy(a_ref, a_in, recv.at[6])
+    fetch_b = pltpu.make_async_copy(view_ref, view_in, recv.at[7])
+    fetch_a.start()
+    fetch_b.start()
 
     barrier = pltpu.get_barrier_semaphore()
 
@@ -89,11 +91,16 @@
 
     greet_across(target, own_target)
     greet_across(source, own_source)
-    greet(ZH, zh, far_block)
+    for step in (1, ZH - 1)[: ZH - 1]:
+        pl.semaphore_signal(barrier, inc=1, device_id=far_block(lax.rem(zh + step, ZH)), device_id_type=MESH)
     greet(M, m, near_chip)
     greet(N, rho, near_row)
+    fetch_b.wait()
+    view_b = view_in[...].astype(f32).T
+    b_ref[...] = jnp.concatenate([view_b[:rows], view_b[rows:]], axis=1).astype(bf16)
+    fetch_a.wait()
     with jax.named_scope("s0_barrier"):
-        pl.semaphore_wait(barrier, 2 * M + (ZH - 1) + (M - 1) + (N - 1) - 2 * own.astype(jnp.int32))
+        pl.semaphore_wait(barrier, 2 * M + min(ZH - 1, 2) + (M - 1) + (N - 1) - 2 * own.astype(jnp.int32))
 
     def spread(n, me, peer, src, dst, i):
         def one(t, c):
@@ -176,7 +183,7 @@
             came(dst, zh, i, 0)
 
     def columns(q):
-        return a_ref.at[:, pl.ds(pl.multiple_of(q * LANES, LANES), LANES)]
+        return a_in.at[:, pl.ds(pl.multiple_of(q * LANES, LANES), LANES)]
 
     across(target, own_target, columns, ta, own_source, 0)
     spread(N, rho, near_row, lambda p: b_ref, pb, 1)
@@ -196,79 +203,85 @@
         g = lax.dot_general(
             normed[own_rows, :], normed[...], (((1,), (1,)), ((), ())), preferred_element_type=f32
         )
-        out[...] = g.reshape(M, SUB, images).astype(bf16)
+        out[:, :, :images] = g.reshape(M, SUB, images).astype(bf16)
+
+    def parts_of(v):
+        high = v.astype(bf16).astype(f32)
+        middle = (v - high).astype(bf16).astype(f32)
+        return tile_of(high, middle, v - high - middle).astype(bf16)
 
     def summed(parts):
         return functools.reduce(jnp.add, [parts[i].astype(f32) for i in range(parts.shape[0])])
 
+    line = lax.broadcasted_iota(jnp.int32, (SUB, LANES), 0)
+
+    def term_of(rg, normed, other):
+        g = rg[...].astype(f32).reshape(rows, images)
+        product = jnp.dot(g.astype(bf16), normed[...], preferred_element_type=f32)
+        return (2.0 * off_weight / images) * product + other * d, g
+
+    def tile_of(*lines):
+        out = jnp.zeros((SUB, LANES), f32)
+        for i, v in enumerate(lines):
+            out = jnp.where(line == i, jnp.broadcast_to(v, out.shape), out)
+        return out
+
+    def projected(term, mine, scaled, first, second):
+        return scaled * (term - first / images - mine * (second / images))
+
     arrived(pb, 1)
-    low = lax.broadcasted_iota(jnp.int32, (rows, LANES), 1) < LANES // 2
+    low = lax.broadcasted_iota(jnp.int32, (rows, LANES), 1) < half
     for i in range(R):
         p0, p1 = pb[2 * i].astype(f32), pb[2 * i + 1].astype(f32)
-        xf[pl.ds(2 * i * rows, rows), :] = jnp.where(low, p0, pltpu.roll(p1, LANES // 2, 1))
-        xf[pl.ds((2 * i + 1) * rows, rows), :] = jnp.where(low, pltpu.roll(p0, LANES // 2, 1), p1)
+        xf[pl.ds(2 * i * rows, rows), :] = jnp.where(low, p0, pltpu.roll(p1, half, 1))
+        xf[pl.ds((2 * i + 1) * rows, rows), :] = jnp.where(low, pltpu.roll(p0, half, 1), p1)
     scaled_b = normalize(nb)
     gram(nb, gp_b)
     spread(M, m, near_chip, lambda p: gp_b.at[p], ra_b, 2)
 
+    arrived(ta, 0)
+    spread(N, rho, near_row, lambda p: ta, xa, 3)
+
     arrived(ra_b, 2)
     hs_b[...] = summed(ra_b).astype(bf16)
     ring_start(hs_b, rb_b, 0)
-
-    arrived(ta, 0)
-    spread(N, rho, near_row, lambda p: ta, xa, 3)
-    for j in range(1, up):
-        ring_step(rb_b, 0, j)
 
     arrived(xa, 3)
     for i in range(N):
         xf[pl.ds(i * rows, rows), :] = xa[i].astype(f32).reshape(rows, LANES)
     scaled_a = normalize(na)
     gram(na, gp_a)
-    spread(M, m, near_chip, lambda p: gp_a.at[p], ra_a, 5)
-
     corr = jnp.sum(na[...].astype(f32) * nb[...].astype(f32), 0, keepdims=True) / images
     d = 2.0 * (corr - 1.0) - (2.0 * off_weight) * corr
-    ds0[...] = jnp.broadcast_to(jnp.square(1.0 - corr) - off_weight * jnp.square(corr), ds0.shape)
-    spread(M, m, near_chip, lambda p: ds0, db0, 6)
-
-    arrived(ra_a, 5)
-    hs_a[...] = summed(ra_a).astype(bf16)
+    parts = parts_of(jnp.square(1.0 - corr) - off_weight * jnp.square(corr))
+    for i in range(M):
+        gp_a[i, :, images:] = parts
+    spread(M, m, near_chip, lambda p: gp_a.at[p], ra_a, 4)
+    mine_a, mine_b = na[own_rows, :].astype(f32), nb[own_rows, :].astype(f32)
+    if up > 1:
+        ring_step(rb_b, 0, 1)
+
+    arrived(ra_a, 4)
+    near = summed(ra_a)
+    hs_a[:, :images] = near[:, :images].astype(bf16)
+    hs_a[:, images:] = parts_of(jnp.sum(near[:, images:], 0, keepdims=True))
     ring_start(hs_a, rb_a, 1)
 
+    for j in range(2, up):
+        ring_step(rb_b, 0, j)
+    if up > 1:
+        ring_step(rb_a, 1, 1)
     ring_step(rb_b, 0, up)
     ms_b[...] = summed(rb_b).astype(bf16)
     spread(M, m, near_chip, lambda p: ms_b, rg_b, 9)
-
-    arrived(db0, 6)
-    ds1[...] = summed(db0)
-    spread(ZH, zh, far_block, lambda p: ds1, db1, 8)
-
-    mine_a, mine_b = na[own_rows, :].astype(f32), nb[own_rows, :].astype(f32)
-    line = lax.broadcasted_iota(jnp.int32, (SUB, LANES), 0)
-    if up > 1:
-        ring_step(rb_a, 1, 1)
-
-    def term_of(rg, normed, other):
-        g = rg[...].astype(f32).reshape(rows, images)
-        product = jnp.dot(g.astype(bf16), normed[...], preferred_element_type=f32)
-        return (2.0 * off_weight / images) * product + other * d, g
-
-    def tile_of(*lines):
-        out = jnp.zeros((SUB, LANES), f32)
-        for i, v in enumerate(lines):
-            out = jnp.where(line == i, jnp.broadcast_to(v, out.shape), out)
-        return out
-
-    def projected(term, mine, scaled, first, second):
-        return scaled * (term - first / images - mine * (second / images))
+    if up > 2:
+        ring_step(rb_a, 1, 2)
 
     arrived(rg_b, 9)
     term_a, g_b = term_of(rg_b, na, mine_b)
     ss_a[...] = tile_of(jnp.sum(term_a, 0, keepdims=True), jnp.sum(term_a * mine_a, 0, keepdims=True))
     spread(N, rho, near_row, lambda p: ss_a, sb_a, 10)
-
-    for j in range(2, up - 1):
+    for j in range(3, up):
         ring_step(rb_a, 1, j)
 
     arrived(sb_a, 10)
@@ -277,40 +290,45 @@
     fs[...] = grad_a.reshape(M, SUB, LANES).astype(bf16)
     across(source, own_source, lambda b: fs.at[b], fa, own_target, 11)
 
-    for j in range(max(up - 1, 2), up):
-        ring_step(rb_a, 1, j)
     ring_step(rb_a, 1, up)
-    ms_a[...] = summed(rb_a).astype(bf16)
+    whole = summed(rb_a)
+    ms_a[...] = whole[:, :images].astype(bf16)
     spread(M, m, near_chip, lambda p: ms_a, rg_a, 12)
+    diagonal = jnp.sum(whole[:, images:], 0, keepdims=True)
+
     arrived(rg_a, 12)
     term_b, g_a = term_of(rg_a, nb, mine_a)
-    both = jnp.sum(g_a * g_b, 0, keepdims=True)
-    trace = functools.reduce(jnp.add, [both[:, i * LANES : (i + 1) * LANES] for i in range(images // LANES)])
-    ss_b[...] = tile_of(
-        jnp.sum(term_b, 0, keepdims=True), jnp.sum(term_b * mine_b, 0, keepdims=True), trace
-    )
-    spread(N, rho, near_row, lambda p: ss_b, sb_b, 13)
-    arrived(sb_b, 13)
-    sums = summed(sb_b)
-    grad_b = projected(term_b, mine_b, scaled_b, sums[0:1], sums[1:2])
-    tb[...] = grad_b.astype(bf16)
+    tb[...] = term_b
     partner = pltpu.make_async_remote_copy(
         src_ref=tb, dst_ref=tp, send_sem=send.at[14], recv_sem=recv.at[14],
         device_id=device(r, z, yh, 1 - k), device_id_type=MESH,
     )
     partner.start()
-
-    arrived(db1, 8)
-    diagonal = summed(db1)[0:1]
-    each = diagonal + sums[2:3] * (off_weight / (images * images))
-    loss_ref[0, 0] = jnp.sum(each) / features
-
+    ss_b[...] = tile_of(jnp.sum(term_b, 0, keepdims=True), jnp.sum(term_b * mine_b, 0, keepdims=True))
+    spread(N, rho, near_row, lambda p: ss_b, sb_b, 13)
+    both = jnp.sum(g_a * g_b, 0, keepdims=True)
+    trace = functools.reduce(jnp.add, [both[:, i * LANES : (i + 1) * LANES] for i in range(images // LANES)])
+    ls[...] = jnp.broadcast_to(trace, ls.shape)
+    spread(N, rho, near_row, lambda p: ls, lb, 8)
+
+    other_rows = pl.ds(pl.multiple_of((r * K + 1 - k) * rows, rows), rows)
     with jax.named_scope("w14"):
         partner.wait()
-    other = tp[...].astype(f32)
-    turned, other_turned = pltpu.roll(grad_b, half, 1), pltpu.roll(other, half, 1)
-    gb_ref[:rows, :] = jnp.where(k == 0, grad_b, other_turned)[:, :half].astype(bf16)
-    gb_ref[rows:, :] = jnp.where(k == 0, other, turned)[:, :half].astype(bf16)
+    other_b, other_mine = tp[...], nb[other_rows, :].astype(f32)
+    arrived(sb_b, 13)
+    sums = summed(sb_b)
+    pieces = [
+        projected(term, mine, scaled_b, sums[0:1], sums[1:2]).T
+        for term, mine in ((term_b, mine_b), (other_b, other_mine))
+    ]
+    own_t, other_t = (jnp.where(k == 0, v[:half], v[half:]) for v in pieces)
+    gb_ref[...] = jnp.where(
+        k == 0, jnp.concatenate([own_t, other_t], axis=1), jnp.concatenate([other_t, own_t], axis=1)
+    ).astype(bf16)
+
+    arrived(lb, 8)
+    each = diagonal + summed(lb)[0:1] * (off_weight / (images * images))
+    loss_ref[0, 0] = jnp.sum(each) / features
 
     arrived(fa, 11)
     for q in range(M):
@@ -318,14 +336,19 @@
 
     sent_across(ta, 0)
     sent_across(fa, 11)
-    for i, dst in ((1, pb), (3, xa), (10, sb_a), (13, sb_b)):
+    for i, dst in ((1, pb), (3, xa), (8, lb), (10, sb_a), (13, sb_b)):
         sent(dst, N - 1, i)
-    for i, dst in ((2, ra_b), (5, ra_a), (6, db0), (9, rg_b), (12, rg_a)):
+    for i, dst in ((2, ra_b), (4, ra_a), (9, rg_b), (12, rg_a)):
         sent(dst, M - 1, i)
     for i, dst in ((0, rb_b), (1, rb_a)):
         part = dst.at[pl.ds(0, ZH - 1)]
         pltpu.make_async_copy(part, part, ring.at[i]).wait()
-    sent(db1, ZH - 1, 8)
+
+
+def hand_over(loss_in, ga_in, gb_in, loss_ref, ga_ref, gb_ref):
+    loss_ref[0, 0] = loss_in[0, 0]
+    ga_ref[...] = ga_in[...]
+    gb_ref[...] = gb_in[...]
 
 
 def solution_on(split, interpret=False):
@@ -338,20 +361,19 @@
 
     def body(view_a, view_b):
         vmem = pltpu.VMEM
+        places = [pl.BlockSpec(memory_space=space) for space in (pltpu.SMEM, pltpu.VMEM, pltpu.VMEM)]
         loss, grad_a, grad_b = pl.pallas_call(
             functools.partial(kernel, X, ZL, YH, ZH),
             out_shape=(
                 jax.ShapeDtypeStruct((1, 1), f32),
                 jax.ShapeDtypeStruct(view_a.shape, bf16),
-                jax.ShapeDtypeStruct(view_b.shape, bf16),
+                jax.ShapeDtypeStruct(view_b.shape[::-1], bf16),
             ),
-            in_specs=[pl.BlockSpec(memory_space=pltpu.VMEM)] * 2,
-            out_specs=[
-                pl.BlockSpec(memory_space=pltpu.SMEM),
-                pl.BlockSpec(memory_space=pltpu.VMEM),
-                pl.BlockSpec(memory_space=pltpu.VMEM),
-            ],
+            in_specs=[pl.BlockSpec(memory_space=pl.ANY)] * 2,
+            out_specs=places,
             scratch_shapes=[
+                vmem(view_a.shape, bf16),
+                vmem(view_b.shape[::-1], bf16),
                 vmem((rows, LANES), bf16),
                 vmem((M, SUB, LANES), bf16),
                 vmem((N, M, SUB, LANES), bf16),
@@ -359,30 +381,28 @@
                 vmem((images, LANES), f32),
                 vmem((images, LANES), bf16),
                 vmem((images, LANES), bf16),
+                vmem((M, SUB, images + LANES), bf16),
                 vmem((M, SUB, images), bf16),
+                vmem((M, SUB, images + LANES), bf16),
                 vmem((M, SUB, images), bf16),
-                vmem((M, SUB, images), bf16),
-                vmem((M, SUB, images), bf16),
+                vmem((SUB, images + LANES), bf16),
                 vmem((SUB, images), bf16),
-                vmem((SUB, images), bf16),
-                vmem((ZH, SUB, images), bf16),
+                vmem((ZH, SUB, images + LANES), bf16),
                 vmem((ZH, SUB, images), bf16),
                 vmem((SUB, images), bf16),
                 vmem((SUB, images), bf16),
                 vmem((M, SUB, images), bf16),
                 vmem((M, SUB, images), bf16),
                 vmem((SUB, LANES), f32),
-                vmem((M, SUB, LANES), f32),
-                vmem((SUB, LANES), f32),
-                vmem((ZH, SUB, LANES), f32),
+                vmem((N, SUB, LANES), f32),
                 vmem((SUB, LANES), f32),
                 vmem((N, SUB, LANES), f32),
                 vmem((SUB, LANES), f32),
                 vmem((N, SUB, LANES), f32),
                 vmem((M, SUB, LANES), bf16),
                 vmem((M, SUB, LANES), bf16),
-                vmem((rows, LANES), bf16),
-                vmem((rows, LANES), bf16),
+                vmem((rows, LANES), f32),
+                vmem((rows, LANES), f32),
                 pltpu.SemaphoreType.DMA((15,)),
                 pltpu.SemaphoreType.DMA((15,)),
                 pltpu.SemaphoreType.DMA((2,)),
@@ -391,7 +411,11 @@
             compiler_params=pltpu.CompilerParams(collective_id=0, has_side_effects=True),
             interpret=interpret,
         )(view_a, view_b.T)
-        return loss.reshape(()), grad_a, grad_b
+        shapes = [jax.ShapeDtypeStruct(v.shape, v.dtype) for v in (loss, grad_a, grad_b)]
+        loss, grad_a, grad_b = pl.pallas_call(
+            hand_over, out_shape=shapes, in_specs=places, out_specs=places, interpret=interpret
+        )(loss, grad_a, grad_b)
+        return loss.reshape(()), grad_a, grad_b.T
 
     return jax.shard_map(
         body,

time: 103 us -> 94.5 us (0.917)
  Pallas kernels: 97.9 us -> 93.6 us
  local copies, waits for them, and re-layouts: 2.07 us -> 0 us
  between operations: 2.41 us -> 0.64 us
    pallas_call x1, Pallas kernels: 97.9 us -> 91.6 us  [body(): pl.pallas_call(functools.partial(kernel, X, ZL, YH, ZH), out_shape=(jax.S...]
    unnamed x4 -> x0, local copies, waits for them, and re-layouts: 2.07 us -> none
    pallas_call x0 -> x1, Pallas kernels: none -> 1.96 us  [body(): pl.pallas_call(hand_over, out_shape=shapes, in_specs=places, out_specs=pl...]
where the time goes in v3:
time: 94.5 us; the launch traced here: 94.2 us
  Pallas kernels  93.6 us (99%)
    pallas_call x1, Pallas kernels, body(): pl.pallas_call(functools.partial(kernel, X, ZL, YH, ZH), out_shape=(jax.S...  91.6 us
    pallas_call x1, Pallas kernels, body(): pl.pallas_call(hand_over, out_shape=shapes, in_specs=places, out_specs=pl...  1.96 us

profile of v3, /device:TPU:1, one launch (start us, length us, event | category | flops | bytes accessed | tf_op | source)
XLA Modules:
  0.0 94.2 jit_solution(5647185253393855676)
XLA Ops:
  0.6 91.6 %shard_map.49 = (f32[1,1]{1,0:T(1,128)}, bf16[8,1024]{1,0:T(8,128)(2,1)}, bf16[64,128]{1,0:T(8,128)(2,1)}) custom-call(bf16[8,1024]{1,0:T(8,128)(2,1)} %a_ref.1, bf16[64,128]{1,0:T(8,128)(2,1)} %bitcast.3), custom_call_target="tpu_custom_call" | custom-call | tf_op jit(solution)/shard_map/pallas_call | solution.py:365
  92.3 2.0 %shard_map.50 = (f32[1,1]{1,0:T(1,128)}, bf16[8,1024]{1,0:T(8,128)(2,1)}, bf16[64,128]{1,0:T(8,128)(2,1)}) custom-call(f32[1,1]{1,0:T(1,128)} %get-tuple-element.9.loss_in, bf16[8,1024]{1,0:T(8,128)(2,1)} %get-tuple-element.10.ga_in, bf16[64,128]{1,0:T(8,128)(2,1)} %get-tuple-element.11.gb_in), custom_call_target="tpu_custom_call" | custom-call | tf_op jit(solution)/shard_map/pallas_call | solution.py:415

commit v4 on v3

--- a/solution.py
+++ b/solution.py
@@ -70,6 +70,11 @@
     fetch_a.start()
     fetch_b.start()
 
+    near_steps = {2: (1,), 4: (2, 1, -1), 8: (2, -2, 1, -1)}[ZH]
+    far_steps = ((2, (2, 1)), (-2, (-1,))) if ZH == 8 else ()
+    seen = {0, *near_steps, *(gone + step for gone, steps in far_steps for step in steps)}
+    seen -= {gone for gone, _ in far_steps}
+
     barrier = pltpu.get_barrier_semaphore()
 
     def greet(n, me, peer):
@@ -91,8 +96,8 @@
 
     greet_across(target, own_target)
     greet_across(source, own_source)
-    for step in (1, ZH - 1)[: ZH - 1]:
-        pl.semaphore_signal(barrier, inc=1, device_id=far_block(lax.rem(zh + step, ZH)), device_id_type=MESH)
+    for step in (1, -1, 2, -2)[: min(ZH // 2 * 2 - 1, 4) if ZH < 8 else 4]:
+        pl.semaphore_signal(barrier, inc=1, device_id=far_block(lax.rem(zh + step + ZH, ZH)), device_id_type=MESH)
     greet(M, m, near_chip)
     greet(N, rho, near_row)
     fetch_b.wait()
@@ -100,7 +105,7 @@
     b_ref[...] = jnp.concatenate([view_b[:rows], view_b[rows:]], axis=1).astype(bf16)
     fetch_a.wait()
     with jax.named_scope("s0_barrier"):
-        pl.semaphore_wait(barrier, 2 * M + min(ZH - 1, 2) + (M - 1) + (N - 1) - 2 * own.astype(jnp.int32))
+        pl.semaphore_wait(barrier, 2 * M + min(ZH - 1, 4) + (M - 1) + (N - 1) - 2 * own.astype(jnp.int32))
 
     def spread(n, me, peer, src, dst, i):
         def one(t, c):
@@ -150,37 +155,35 @@
         def _():
             sent(dst, M, i)
 
-    up, down = ZH // 2, ZH - 1 - ZH // 2
-
-    def pass_on(src, dst, slot, i, j, step):
+    def block(step):
+        return lax.rem(zh + step + ZH, ZH)
+
+    def pass_on(src, dst, i, step, gone):
         pltpu.make_async_remote_copy(
-            src_ref=src, dst_ref=dst.at[slot], send_sem=ring.at[i], recv_sem=hop.at[i, j],
-            device_id=far_block(lax.rem(zh + step + ZH, ZH)), device_id_type=MESH,
+            src_ref=src, dst_ref=dst.at[block(step - (step + gone))], send_sem=ring.at[i],
+            recv_sem=hop.at[i, (step + gone) % ZH], device_id=far_block(block(step)), device_id_type=MESH,
         ).start()
 
-    def came(dst, slot, i, j):
-        with jax.named_scope(f"h{i}_{j}"):
-            pltpu.make_async_copy(dst.at[slot], dst.at[slot], hop.at[i, j]).wait()
-
-    def ring_start(src, dst, i):
+    def came(dst, i, gone):
+        with jax.named_scope(f"h{i}_{gone % ZH}"):
+            slot = dst.at[block(-gone)]
+            pltpu.make_async_copy(slot, slot, hop.at[i, gone % ZH]).wait()
+
+    def blocks_start(src, dst, i):
         pltpu.make_async_copy(src, dst.at[zh], hop.at[i, 0]).start()
-        pass_on(src, dst, zh, i, 1, 1)
-        if down:
-            pass_on(src, dst, zh, i, up + 1, -1)
-
-    def ring_step(dst, i, j):
-        if j <= up:
-            slot = lax.rem(zh - j + ZH, ZH)
-            came(dst, slot, i, j)
-            if j < up:
-                pass_on(dst.at[slot], dst, slot, i, j + 1, 1)
-        if j <= down:
-            slot = lax.rem(zh + j, ZH)
-            came(dst, slot, i, up + j)
-            if j < down:
-                pass_on(dst.at[slot], dst, slot, i, up + j + 1, -1)
-        if j == up:
-            came(dst, zh, i, 0)
+        for step in near_steps:
+            pass_on(src, dst, i, step, 0)
+
+    def blocks_forward(dst, i):
+        for gone, steps in far_steps:
+            came(dst, i, gone)
+            for step in steps:
+                pass_on(dst.at[block(-gone)], dst, i, step, gone)
+
+    def blocks_end(dst, i):
+        for gone in (0, *(g for g in (1, -1, 2, 3, 4, -3) if g % ZH and abs(g) <= ZH // 2)):
+            if gone in seen:
+                came(dst, i, gone)
 
     def columns(q):
         return a_in.at[:, pl.ds(pl.multiple_of(q * LANES, LANES), LANES)]
@@ -244,7 +247,7 @@
 
     arrived(ra_b, 2)
     hs_b[...] = summed(ra_b).astype(bf16)
-    ring_start(hs_b, rb_b, 0)
+    blocks_start(hs_b, rb_b, 0)
 
     arrived(xa, 3)
     for i in range(N):
@@ -258,43 +261,35 @@
         gp_a[i, :, images:] = parts
     spread(M, m, near_chip, lambda p: gp_a.at[p], ra_a, 4)
     mine_a, mine_b = na[own_rows, :].astype(f32), nb[own_rows, :].astype(f32)
-    if up > 1:
-        ring_step(rb_b, 0, 1)
+    blocks_forward(rb_b, 0)
 
     arrived(ra_a, 4)
     near = summed(ra_a)
     hs_a[:, :images] = near[:, :images].astype(bf16)
     hs_a[:, images:] = parts_of(jnp.sum(near[:, images:], 0, keepdims=True))
-    ring_start(hs_a, rb_a, 1)
-
-    for j in range(2, up):
-        ring_step(rb_b, 0, j)
-    if up > 1:
-        ring_step(rb_a, 1, 1)
-    ring_step(rb_b, 0, up)
+    blocks_start(hs_a, rb_a, 1)
+
+    blocks_end(rb_b, 0)
     ms_b[...] = summed(rb_b).astype(bf16)
     spread(M, m, near_chip, lambda p: ms_b, rg_b, 9)
-    if up > 2:
-        ring_step(rb_a, 1, 2)
+    blocks_forward(rb_a, 1)
 
     arrived(rg_b, 9)
     term_a, g_b = term_of(rg_b, na, mine_b)
     ss_a[...] = tile_of(jnp.sum(term_a, 0, keepdims=True), jnp.sum(term_a * mine_a, 0, keepdims=True))
     spread(N, rho, near_row, lambda p: ss_a, sb_a, 10)
-    for j in range(3, up):
-        ring_step(rb_a, 1, j)
+
+    blocks_end(rb_a, 1)
+    whole = summed(rb_a)
+    ms_a[...] = whole[:, :images].astype(bf16)
+    spread(M, m, near_chip, lambda p: ms_a, rg_a, 12)
+    diagonal = jnp.sum(whole[:, images:], 0, keepdims=True)
 
     arrived(sb_a, 10)
     sums = summed(sb_a)
     grad_a = projected(term_a, mine_a, scaled_a, sums[0:1], sums[1:2])
     fs[...] = grad_a.reshape(M, SUB, LANES).astype(bf16)
     across(source, own_source, lambda b: fs.at[b], fa, own_target, 11)
-
-    ring_step(rb_a, 1, up)
-    whole = summed(rb_a)
-    ms_a[...] = whole[:, :images].astype(bf16)
-    spread(M, m, near_chip, lambda p: ms_a, rg_a, 12)
-    diagonal = jnp.sum(whole[:, images:], 0, keepdims=True)
 
     arrived(rg_a, 12)
     term_b, g_a = term_of(rg_a, nb, mine_a)

time: 94.5 us -> 91.1 us (0.964)
  Pallas kernels: 93.6 us -> 90.3 us
    pallas_call x1, Pallas kernels: 91.6 us -> 88.3 us  [body(): pl.pallas_call(functools.partial(kernel, X, ZL, YH, ZH), out_shape=(jax.S...]
where the time goes in v4:
time: 91.1 us; the launch traced here: 90.9 us
  Pallas kernels  90.3 us (99%)
    pallas_call x1, Pallas kernels, body(): pl.pallas_call(functools.partial(kernel, X, ZL, YH, ZH), out_shape=(jax.S...  88.3 us
    pallas_call x1, Pallas kernels, body(): pl.pallas_call(hand_over, out_shape=shapes, in_specs=places, out_specs=pl...  1.96 us

profile of v4, /device:TPU:1, one launch (start us, length us, event | category | flops | bytes accessed | tf_op | source)
XLA Modules:
  0.0 90.9 jit_solution(17569177403106385323)
XLA Ops:
  0.6 88.3 %shard_map.49 = (f32[1,1]{1,0:T(1,128)}, bf16[8,1024]{1,0:T(8,128)(2,1)}, bf16[64,128]{1,0:T(8,128)(2,1)}) custom-call(bf16[8,1024]{1,0:T(8,128)(2,1)} %a_ref.1, bf16[64,128]{1,0:T(8,128)(2,1)} %bitcast.3), custom_call_target="tpu_custom_call" | custom-call | tf_op jit(solution)/shard_map/pallas_call | solution.py:360
  88.9 2.0 %shard_map.50 = (f32[1,1]{1,0:T(1,128)}, bf16[8,1024]{1,0:T(8,128)(2,1)}, bf16[64,128]{1,0:T(8,128)(2,1)}) custom-call(f32[1,1]{1,0:T(1,128)} %get-tuple-element.9.loss_in, bf16[8,1024]{1,0:T(8,128)(2,1)} %get-tuple-element.10.ga_in, bf16[64,128]{1,0:T(8,128)(2,1)} %get-tuple-element.11.gb_in), custom_call_target="tpu_custom_call" | custom-call | tf_op jit(solution)/shard_map/pallas_call | solution.py:410

commit v5 on v4

--- a/solution.py
+++ b/solution.py
@@ -29,7 +29,7 @@
     a_in, view_in, b_ref, ta, xa, pb, xf, na, nb,
     gp_a, gp_b, ra_a, ra_b, hs_a, hs_b, rb_a, rb_b, ms_a, ms_b, rg_a, rg_b,
     ss_a, sb_a, ss_b, sb_b, ls, lb, fs, fa, tb, tp,
-    send, recv, ring, hop,
+    send, recv, ring, hop, pair,
 ):
     R, M = ZH, ZL * YH
     N = R * K
@@ -71,9 +71,7 @@
     fetch_b.start()
 
     near_steps = {2: (1,), 4: (2, 1, -1), 8: (2, -2, 1, -1)}[ZH]
-    far_steps = ((2, (2, 1)), (-2, (-1,))) if ZH == 8 else ()
-    seen = {0, *near_steps, *(gone + step for gone, steps in far_steps for step in steps)}
-    seen -= {gone for gone, _ in far_steps}
+    last = {2: (0, 1), 4: (0, 2, 1, -1), 8: (0, 1, -1, 3, -3, 4)}[ZH]
 
     barrier = pltpu.get_barrier_semaphore()
 
@@ -127,6 +125,19 @@
         part = dst.at[pl.ds(0, n)]
         pltpu.make_async_copy(part, part, send.at[i]).wait()
 
+    def gather(src, dst, i):
+        spread(R, r, lambda p: device(p, z, yh, k), lambda p: src, dst.at[k], i)
+
+    def swap(dst, i, j):
+        arrived(dst.at[k], i)
+        copy = pltpu.make_async_remote_copy(
+            src_ref=dst.at[k], dst_ref=dst.at[k], send_sem=pair.at[j], recv_sem=pair.at[j + 1],
+            device_id=device(r, z, yh, 1 - k), device_id_type=MESH,
+        )
+        copy.start()
+        with jax.named_scope(f"x{i}"):
+            copy.wait()
+
     def across(peer, own_index, src, dst, slot, i):
         def one(q, c):
             mine = jnp.logical_and(own, q == own_index)
@@ -158,12 +169,6 @@
     def block(step):
         return lax.rem(zh + step + ZH, ZH)
 
-    def pass_on(src, dst, i, step, gone):
-        pltpu.make_async_remote_copy(
-            src_ref=src, dst_ref=dst.at[block(step - (step + gone))], send_sem=ring.at[i],
-            recv_sem=hop.at[i, (step + gone) % ZH], device_id=far_block(block(step)), device_id_type=MESH,
-        ).start()
-
     def came(dst, i, gone):
         with jax.named_scope(f"h{i}_{gone % ZH}"):
             slot = dst.at[block(-gone)]
@@ -172,24 +177,37 @@
     def blocks_start(src, dst, i):
         pltpu.make_async_copy(src, dst.at[zh], hop.at[i, 0]).start()
         for step in near_steps:
-            pass_on(src, dst, i, step, 0)
+            pltpu.make_async_remote_copy(
+                src_ref=src, dst_ref=dst.at[zh], send_sem=ring.at[i], recv_sem=hop.at[i, step % ZH],
+                device_id=far_block(block(step)), device_id_type=MESH,
+            ).start()
+
+    def hand_on(slot, i, step, mark):
+        pltpu.make_async_remote_copy(
+            src_ref=slot, dst_ref=slot, send_sem=ring.at[i], recv_sem=hop.at[i, mark],
+            device_id=far_block(block(step)), device_id_type=MESH,
+        ).start()
 
     def blocks_forward(dst, i):
-        for gone, steps in far_steps:
+        if ZH < 8:
+            return
+        for nth, turn in enumerate((1 - 2 * k, 2 * k - 1)):
+            slot = dst.at[block(-2 * turn)]
+            with jax.named_scope(f"f{i}"):
+                pltpu.make_async_copy(slot, slot, hop.at[i, lax.rem(2 * turn + ZH, ZH)]).wait()
+            if nth == 0:
+                hand_on(slot, i, 2 * turn, 4)
+            hand_on(slot, i, turn, lax.rem(3 * turn + ZH, ZH))
+
+    def blocks_end(dst, i):
+        for gone in last:
             came(dst, i, gone)
-            for step in steps:
-                pass_on(dst.at[block(-gone)], dst, i, step, gone)
-
-    def blocks_end(dst, i):
-        for gone in (0, *(g for g in (1, -1, 2, 3, 4, -3) if g % ZH and abs(g) <= ZH // 2)):
-            if gone in seen:
-                came(dst, i, gone)
 
     def columns(q):
         return a_in.at[:, pl.ds(pl.multiple_of(q * LANES, LANES), LANES)]
 
     across(target, own_target, columns, ta, own_source, 0)
-    spread(N, rho, near_row, lambda p: b_ref, pb, 1)
+    gather(b_ref, pb, 1)
 
     def normalize(normed):
         values = xf[...]
@@ -232,10 +250,10 @@
     def projected(term, mine, scaled, first, second):
         return scaled * (term - first / images - mine * (second / images))
 
-    arrived(pb, 1)
+    swap(pb, 1, 0)
     low = lax.broadcasted_iota(jnp.int32, (rows, LANES), 1) < half
     for i in range(R):
-        p0, p1 = pb[2 * i].astype(f32), pb[2 * i + 1].astype(f32)
+        p0, p1 = pb[0, i].astype(f32), pb[1, i].astype(f32)
         xf[pl.ds(2 * i * rows, rows), :] = jnp.where(low, p0, pltpu.roll(p1, half, 1))
         xf[pl.ds((2 * i + 1) * rows, rows), :] = jnp.where(low, pltpu.roll(p0, half, 1), p1)
     scaled_b = normalize(nb)
@@ -243,15 +261,15 @@
     spread(M, m, near_chip, lambda p: gp_b.at[p], ra_b, 2)
 
     arrived(ta, 0)
-    spread(N, rho, near_row, lambda p: ta, xa, 3)
+    gather(ta, xa, 3)
 
     arrived(ra_b, 2)
     hs_b[...] = summed(ra_b).astype(bf16)
     blocks_start(hs_b, rb_b, 0)
 
-    arrived(xa, 3)
+    swap(xa, 3, 2)
     for i in range(N):
-        xf[pl.ds(i * rows, rows), :] = xa[i].astype(f32).reshape(rows, LANES)
+        xf[pl.ds(i * rows, rows), :] = xa[i % K, i // K].astype(f32).reshape(rows, LANES)
     scaled_a = normalize(na)
     gram(na, gp_a)
     corr = jnp.sum(na[...].astype(f32) * nb[...].astype(f32), 0, keepdims=True) / images
@@ -331,7 +349,9 @@
 
     sent_across(ta, 0)
     sent_across(fa, 11)
-    for i, dst in ((1, pb), (3, xa), (8, lb), (10, sb_a), (13, sb_b)):
+    for i, dst in ((1, pb), (3, xa)):
+        sent(dst.at[0], R - 1, i)
+    for i, dst in ((8, lb), (10, sb_a), (13, sb_b)):
         sent(dst, N - 1, i)
     for i, dst in ((2, ra_b), (4, ra_a), (9, rg_b), (12, rg_a)):
         sent(dst, M - 1, i)
@@ -361,8 +381,8 @@
             functools.partial(kernel, X, ZL, YH, ZH),
             out_shape=(
                 jax.ShapeDtypeStruct((1, 1), f32),
-                jax.ShapeDtypeStruct(view_a.shape, bf16),
-                jax.ShapeDtypeStruct(view_b.shape[::-1], bf16),
+                vmem(view_a.shape, bf16),
+                vmem(view_b.shape[::-1], bf16),
             ),
             in_specs=[pl.BlockSpec(memory_space=pl.ANY)] * 2,
             out_specs=places,
@@ -371,8 +391,8 @@
                 vmem(view_b.shape[::-1], bf16),
                 vmem((rows, LANES), bf16),
                 vmem((M, SUB, LANES), bf16),
-                vmem((N, M, SUB, LANES), bf16),
-                vmem((N, rows, LANES), bf16),
+                vmem((K, R, M, SUB, LANES), bf16),
+                vmem((K, R, rows, LANES), bf16),
                 vmem((images, LANES), f32),
                 vmem((images, LANES), bf16),
                 vmem((images, LANES), bf16),
@@ -402,6 +422,7 @@
                 pltpu.SemaphoreType.DMA((15,)),
                 pltpu.SemaphoreType.DMA((2,)),
                 pltpu.SemaphoreType.DMA((2, ZH)),
+                pltpu.SemaphoreType.DMA((4,)),
             ],
             compiler_params=pltpu.CompilerParams(collective_id=0, has_side_effects=True),
             interpret=interpret,
@@ -409,7 +430,7 @@
         shapes = [jax.ShapeDtypeStruct(v.shape, v.dtype) for v in (loss, grad_a, grad_b)]
         loss, grad_a, grad_b = pl.pallas_call(
             hand_over, out_shape=shapes, in_specs=places, out_specs=places, interpret=interpret
-        )(loss, grad_a, grad_b)
+        )(loss, *(pltpu.with_memory_space_constraint(v, pltpu.VMEM) for v in (grad_a, grad_b)))
         return loss.reshape(()), grad_a, grad_b.T
 
     return jax.shard_map(

time: 91.1 us -> 89 us (0.977)
  Pallas kernels: 90.3 us -> 88.2 us
    pallas_call x1, Pallas kernels: 88.3 us -> 87 us  [body(): pl.pallas_call(functools.partial(kernel, X, ZL, YH, ZH), out_shape=(jax.S...]
where the time goes in v5:
time: 89 us; the launch traced here: 88.8 us
  Pallas kernels  88.2 us (99%)
    pallas_call x1, Pallas kernels, body(): pl.pallas_call(functools.partial(kernel, X, ZL, YH, ZH), out_shape=(jax.S...  87 us

profile of v5, /device:TPU:1, one launch (start us, length us, event | category | flops | bytes accessed | tf_op | source)
XLA Modules:
  0.0 88.8 jit_solution(17884209687791312005)
XLA Ops:
  0.6 87.0 %shard_map.49 = (f32[1,1]{1,0:T(1,128)}, bf16[8,1024]{1,0:T(8,128)(2,1)S(1)}, bf16[64,128]{1,0:T(8,128)(2,1)S(1)}) custom-call(bf16[8,1024]{1,0:T(8,128)(2,1)} %a_ref.1, bf16[64,128]{1,0:T(8,128)(2,1)} %bitcast.3), custom_call_target="tpu_custom_call" | custom-call | tf_op jit(solution)/shard_map/pallas_call | solution.py:380
  87.6 1.3 %shard_map.50 = (f32[1,1]{1,0:T(1,128)}, bf16[8,1024]{1,0:T(8,128)(2,1)}, bf16[64,128]{1,0:T(8,128)(2,1)}) custom-call(f32[1,1]{1,0:T(1,128)} %get-tuple-element.9.loss_in, bf16[8,1024]{1,0:T(8,128)(2,1)S(1)} %get-tuple-element.10.ga_in, bf16[64,128]{1,0:T(8,128)(2,1)S(1)} %get-tuple-element.11.gb_in), custom_call_target="tpu_custom_call" | custom-call | tf_op jit(solution)/shard_map/pallas_call | solution.py:431

commit v6 on v5

--- a/solution.py
+++ b/solution.py
@@ -247,6 +247,9 @@
             out = jnp.where(line == i, jnp.broadcast_to(v, out.shape), out)
         return out
 
+    def sums_of(term, mine):
+        return jnp.concatenate([jnp.sum(v, 0, keepdims=True) for v in (term, term * mine)], axis=0)
+
     def projected(term, mine, scaled, first, second):
         return scaled * (term - first / images - mine * (second / images))
 
@@ -294,7 +297,7 @@
 
     arrived(rg_b, 9)
     term_a, g_b = term_of(rg_b, na, mine_b)
-    ss_a[...] = tile_of(jnp.sum(term_a, 0, keepdims=True), jnp.sum(term_a * mine_a, 0, keepdims=True))
+    ss_a[...] = sums_of(term_a, mine_a)
     spread(N, rho, near_row, lambda p: ss_a, sb_a, 10)
 
     blocks_end(rb_a, 1)
@@ -317,11 +320,11 @@
         device_id=device(r, z, yh, 1 - k), device_id_type=MESH,
     )
     partner.start()
-    ss_b[...] = tile_of(jnp.sum(term_b, 0, keepdims=True), jnp.sum(term_b * mine_b, 0, keepdims=True))
+    ss_b[...] = sums_of(term_b, mine_b)
     spread(N, rho, near_row, lambda p: ss_b, sb_b, 13)
     both = jnp.sum(g_a * g_b, 0, keepdims=True)
     trace = functools.reduce(jnp.add, [both[:, i * LANES : (i + 1) * LANES] for i in range(images // LANES)])
-    ls[...] = jnp.broadcast_to(trace, ls.shape)
+    ls[...] = trace
     spread(N, rho, near_row, lambda p: ls, lb, 8)
 
     other_rows = pl.ds(pl.multiple_of((r * K + 1 - k) * rows, rows), rows)
@@ -343,10 +346,6 @@
     each = diagonal + summed(lb)[0:1] * (off_weight / (images * images))
     loss_ref[0, 0] = jnp.sum(each) / features
 
-    arrived(fa, 11)
-    for q in range(M):
-        ga_ref[:, q * LANES : (q + 1) * LANES] = fa[q]
-
     sent_across(ta, 0)
     sent_across(fa, 11)
     for i, dst in ((1, pb), (3, xa)):
@@ -358,6 +357,10 @@
     for i, dst in ((0, rb_b), (1, rb_a)):
         part = dst.at[pl.ds(0, ZH - 1)]
         pltpu.make_async_copy(part, part, ring.at[i]).wait()
+
+    arrived(fa, 11)
+    for q in range(M):
+        ga_ref[:, q * LANES : (q + 1) * LANES] = fa[q]
 
 
 def hand_over(loss_in, ga_in, gb_in, loss_ref, ga_ref, gb_ref):
@@ -408,12 +411,12 @@
                 vmem((SUB, images), bf16),
                 vmem((M, SUB, images), bf16),
                 vmem((M, SUB, images), bf16),
-                vmem((SUB, LANES), f32),
-                vmem((N, SUB, LANES), f32),
-                vmem((SUB, LANES), f32),
-                vmem((N, SUB, LANES), f32),
-                vmem((SUB, LANES), f32),
-                vmem((N, SUB, LANES), f32),
+                vmem((2, LANES), f32),
+                vmem((N, 2, LANES), f32),
+                vmem((2, LANES), f32),
+                vmem((N, 2, LANES), f32),
+                vmem((1, LANES), f32),
+                vmem((N, 1, LANES), f32),
                 vmem((M, SUB, LANES), bf16),
                 vmem((M, SUB, LANES), bf16),
                 vmem((rows, LANES), f32),

time: 89 us -> 88.7 us (level)
  no operation moved by 1% of the time
where the time goes in v6:
time: 88.7 us; the launch traced here: 88.5 us
  Pallas kernels  87.9 us (99%)
    pallas_call x1, Pallas kernels, body(): pl.pallas_call(functools.partial(kernel, X, ZL, YH, ZH), out_shape=(jax.S...  86.7 us

profile of v6, /device:TPU:1, one launch (start us, length us, event | category | flops | bytes accessed | tf_op | source)
XLA Modules:
  0.0 88.5 jit_solution(7601519896347055005)
XLA Ops:
  0.6 86.7 %shard_map.49 = (f32[1,1]{1,0:T(1,128)}, bf16[8,1024]{1,0:T(8,128)(2,1)S(1)}, bf16[64,128]{1,0:T(8,128)(2,1)S(1)}) custom-call(bf16[8,1024]{1,0:T(8,128)(2,1)} %a_ref.1, bf16[64,128]{1,0:T(8,128)(2,1)} %bitcast.3), custom_call_target="tpu_custom_call" | custom-call | tf_op jit(solution)/shard_map/pallas_call | solution.py:383
  87.3 1.3 %shard_map.50 = (f32[1,1]{1,0:T(1,128)}, bf16[8,1024]{1,0:T(8,128)(2,1)}, bf16[64,128]{1,0:T(8,128)(2,1)}) custom-call(f32[1,1]{1,0:T(1,128)} %get-tuple-element.9.loss_in, bf16[8,1024]{1,0:T(8,128)(2,1)S(1)} %get-tuple-element.10.ga_in, bf16[64,128]{1,0:T(8,128)(2,1)S(1)} %get-tuple-element.11.gb_in), custom_call_target="tpu_custom_call" | custom-call | tf_op jit(solution)/shard_map/pallas_call | solution.py:434
